TPU v7x, 32 devices: a whole 2x2x4 slice. The times are simulated.
32 devices in a mesh: circ: 8 (over z, x), cell: 4 (over y, core).
Axes of the slice: x: 2, y: 2, z: 4, core: 2. Of those that a mesh axis runs over, the one named last changes fastest.
Arguments:
- flow_state: bfloat16 [35, 8, 16, 1024], P(None, 'circ', 'cell'), may hold values from -6 to 6
- time_coef: float32 [8, 16, 1024], P('circ', 'cell'), may hold values from 0.3 to 3
- axial_damp: bfloat16 [8, 16, 1024], P('circ', 'cell'), may hold values from 0.19921875 to 2
- plane_damp: bfloat16 [8, 16, 2048], P('circ', 'cell'), may hold values from 0.19921875 to 2
- periodic_damp: bfloat16 [8, 16, 64], P('circ', 'cell'), may hold values from 0.19921875 to 2
- flux_jacobian: float32 [3, 5, 5], replicated, may hold values from -2.5 to 2.5
- face_cells: int32 [2, 2048], replicated, may hold values from 0 to 1023, as said below
- periodic_cells: int32 [2, 64], replicated, may hold values from 0 to 1023, as said below
- face_map: int32 [64], replicated, may hold values from 0 to 63, each once
- wall_cells: int32 [1024], P('cell'), may hold values from 0 to 4095, as said below
- wall_normals: float32 [3, 1024], P(None, 'cell'), may hold values from -6 to 6
- pressure_weights: float32 [5], replicated, may hold values from -4 to 4
- mode_shapes: float32 [2, 8, 3, 400], replicated, may hold values from -0.00390625 to 0.00390625
Outputs:
- jacobian_image: bfloat16 [35, 8, 16, 1024], P(None, 'circ', 'cell')
- modal_forces: float32 [7, 400], replicated
Inputs may be any that keep to these rules, and one draw needn't show every extreme that they name: `face_cells`: each column names the two cells of a layer that one in-plane face joins; the two differ. `periodic_cells`: all 128 entries differ. `face_map`: each value of 0 to 63 once. `wall_cells`: an entry is the wall cell's layer within its cell block times 1024 plus its cell in the layer; entries may repeat.
All inputs are finite; a program needn't handle non-finite values.
Results may differ from a plain program's by a relative error of at most 0.0055.
Values may be sent and summed in bfloat16 or wider, within the bound.
A program may use at most 64 MiB of HBM per device.

v0:
```python
import math
import jax
import jax.numpy as jnp
import numpy as np
from jax import lax
from jax.sharding import PartitionSpec as P

NV = 5
HB = 7


def shifted(value, axis, steps):
    count = lax.axis_size(axis)
    first, last = (max(0, -steps), min(count, count - steps))
    return lax.ppermute(value, axis, [(source, source + steps) for source in range(first, last)])


def shifted_2(value, axis, steps):
    count = lax.axis_size(axis)
    pairs = [(source, (source + steps) % count) for source in range(count)]
    return lax.ppermute(value, axis, pairs)


def harmonic_matrix(instances):
    matrix_table = np.zeros((instances, instances))
    for row_index in range(instances):
        for column_index in range(instances):
            if row_index != column_index:
                offset_steps = row_index - column_index
                matrix_table[row_index, column_index] = (
                    0.5 * (-1.0) ** offset_steps / math.sin(math.pi * offset_steps / instances)
                )
    return matrix_table


def face_flux(jacobian, damping, lower_state, upper_state):
    total_state = lower_state + upper_state
    jump_state = upper_state - lower_state
    convected = jnp.einsum(
        "vw,nw...->nv...", jacobian, total_state, precision=lax.Precision.HIGHEST
    )
    return 0.5 * convected - 0.5 * damping * jump_state


def column_table(index_list, count):
    return (lax.iota(jnp.int32, count)[:, None] == index_list[None, :]).astype(jnp.bfloat16)


def take_columns(values, table):
    leading = values.shape[:-1]
    flat_values = values.reshape(-1, values.shape[-1])
    picked = jnp.dot(flat_values, table, preferred_element_type=jnp.float32)
    return picked.reshape(leading + (table.shape[1],))


def spread_columns(terms, table):
    leading = terms.shape[:-1]
    flat_terms = terms.reshape(-1, terms.shape[-1])
    high_part = flat_terms.astype(jnp.bfloat16)
    rest_one = flat_terms - high_part.astype(jnp.float32)
    middle_part = rest_one.astype(jnp.bfloat16)
    low_part = (rest_one - middle_part.astype(jnp.float32)).astype(jnp.bfloat16)
    contract = (((1,), (1,)), ((), ()))
    spread = lax.dot_general(high_part, table, contract, preferred_element_type=jnp.float32)
    spread = spread + lax.dot_general(
        middle_part, table, contract, preferred_element_type=jnp.float32
    )
    spread = spread + lax.dot_general(low_part, table, contract, preferred_element_type=jnp.float32)
    return spread.reshape(leading + (table.shape[0],))


def project_all(all_forces, mode_shapes, passages, angle_step, diameters):
    phase_index = (diameters[:, None] * diameters[None, :] % passages).astype(jnp.float32)
    cosine_table = jnp.cos(angle_step * phase_index)
    sine_table = jnp.sin(angle_step * phase_index)
    real_part = jnp.einsum("dp,pkn->dkn", cosine_table, all_forces, precision=lax.Precision.HIGHEST)
    imag_part = -jnp.einsum("dp,pkn->dkn", sine_table, all_forces, precision=lax.Precision.HIGHEST)
    return jnp.einsum(
        "dkm,dkn->nm", mode_shapes[0], real_part, precision=lax.Precision.HIGHEST
    ) + jnp.einsum("dkm,dkn->nm", mode_shapes[1], imag_part, precision=lax.Precision.HIGHEST)


def shards(
    flow_state,
    time_coef,
    axial_damp,
    plane_damp,
    periodic_damp,
    flux_jacobian,
    face_cells,
    periodic_cells,
    face_map,
    wall_cells,
    wall_normals,
    pressure_weights,
    mode_shapes,
):
    layers = flow_state.shape[2]
    plane_cells = flow_state.shape[3]
    passages = lax.axis_size("circ")
    state_narrow = flow_state.reshape(HB, NV, layers, plane_cells)
    current = state_narrow.astype(jnp.float32)
    harmonic = jnp.asarray(harmonic_matrix(HB), jnp.float32)
    jacobian_sum = time_coef[0][None, None] * jnp.einsum(
        "nm,mvac->nvac", harmonic, current, precision=lax.Precision.HIGHEST
    )
    cell_ids = lax.iota(jnp.int32, plane_cells)[:, None]
    owner_hits = cell_ids == face_cells[0][None, :]
    neighbour_hits = cell_ids == face_cells[1][None, :]
    owner_table = owner_hits.astype(jnp.bfloat16)
    neighbour_table = neighbour_hits.astype(jnp.bfloat16)
    signed_table = (owner_hits.astype(jnp.int32) - neighbour_hits.astype(jnp.int32)).astype(
        jnp.bfloat16
    )
    owner_values = take_columns(state_narrow, owner_table)
    neighbour_values = take_columns(state_narrow, neighbour_table)
    plane_flux = face_flux(
        flux_jacobian[1], plane_damp[0].astype(jnp.float32), owner_values, neighbour_values
    )
    jacobian_sum = jacobian_sum + spread_columns(plane_flux, signed_table)
    above_layer = shifted(state_narrow[:, :, :1], "cell", -1)
    upper_rows = jnp.concatenate([current[:, :, 1:], above_layer.astype(jnp.float32)], axis=2)
    own_flux = face_flux(flux_jacobian[0], axial_damp[0].astype(jnp.float32), current, upper_rows)
    zero_layer = jnp.zeros((HB, NV, 1, plane_cells), jnp.float32)
    jacobian_sum = (
        jacobian_sum + own_flux - jnp.concatenate([zero_layer, own_flux[:, :, :-1]], axis=2)
    )
    from_below = shifted(own_flux[:, :, -1:].astype(jnp.bfloat16), "cell", 1).astype(jnp.float32)
    jacobian_sum = jacobian_sum - jnp.concatenate(
        [from_below, jnp.zeros((HB, NV, layers - 1, plane_cells), jnp.float32)], axis=2
    )
    lower_side = periodic_cells[0]
    upper_side = periodic_cells[1]
    targets = lower_side[face_map]
    upper_table = column_table(upper_side, plane_cells)
    target_table = column_table(targets, plane_cells)
    own_targets = take_columns(state_narrow, target_table)
    own_upper = take_columns(state_narrow, upper_table)
    next_lower = shifted_2(own_targets.astype(jnp.bfloat16), "circ", -1)
    matched_next = next_lower.astype(jnp.float32)
    periodic_own = face_flux(
        flux_jacobian[2], periodic_damp[0].astype(jnp.float32), own_upper, matched_next
    )
    from_previous = shifted_2(periodic_own.astype(jnp.bfloat16), "circ", 1).astype(
        periodic_own.dtype
    )
    side_terms = jnp.concatenate([periodic_own, -from_previous], axis=3)
    side_table = jnp.concatenate([upper_table, target_table], axis=1)
    jacobian_sum = jacobian_sum + spread_columns(side_terms, side_table)
    jacobian_image = jacobian_sum.astype(jnp.bfloat16).reshape(HB * NV, 1, layers, plane_cells)
    flat_state = state_narrow.reshape(HB, NV, layers * plane_cells)
    wall_table = column_table(wall_cells, layers * plane_cells)
    wall_state = take_columns(flat_state, wall_table)
    wall_pressure = jnp.einsum(
        "v,nvw->nw", pressure_weights, wall_state, precision=lax.Precision.HIGHEST
    )
    block_force = jnp.einsum(
        "kw,nw->kn", wall_normals, wall_pressure, precision=lax.Precision.HIGHEST
    )
    angle_step = 2.0 * math.pi / passages
    diameters = lax.iota(jnp.int32, passages)
    passage_force = lax.psum(block_force, "cell")
    all_forces = lax.all_gather(passage_force[None], "circ", axis=0, tiled=True)
    modal_forces = project_all(all_forces, mode_shapes, passages, angle_step, diameters)
    return (jacobian_image, modal_forces)


def solution(mesh):
    placed = (
        P(None, "circ", "cell", None),
        P("circ", "cell", None),
        P("circ", "cell", None),
        P("circ", "cell", None),
        P("circ", "cell", None),
        P(),
        P(),
        P(),
        P(),
        P("cell"),
        P(None, "cell"),
        P(),
        P(),
    )
    return jax.shard_map(
        shards,
        mesh=mesh,
        in_specs=placed,
        out_specs=(P(None, "circ", "cell", None), P()),
        check_vma=False,
    )
```

profile of v0, /device:TPU:1, one launch (start us, length us, event | category | flops | bytes accessed | tf_op | source)
XLA Modules:
  0.0 93.3 jit_solution(8377886405390207188)
XLA Ops:
  0.7 1.1 %reshape_reshape.2 = bf16[140,1024]{1,0:T(8,128)(2,1)S(1)} reshape(bf16[35,1,4,1024]{3,2,1,0:T(4,128)(2,1)} %param.14) | data formatting | bytes 573440 | tf_op jit(solution)/shard_map/reshape;reshape | solution.py:51
  1.8 0.8 slice_bitcast_fusion.1
  2.5 0.7 compare_select_fusion
  3.2 0.8 gather_fusion
  4.0 0.3 fusion.26
  4.4 0.6 copy.68
  5.0 5.1 %collective-permute-start.2 = (bf16[7,5,4,64]{3,1,2,0:T(8,128)(2,1)}, bf16[7,5,4,64]{3,1,2,0:T(8,128)(2,1)}, u32[]{:S(2)}, u32[]{:S(2)}) collective-permute-start(bf16[7,5,4,64]{3,1,2,0:T(8,128)(2,1)} %copy.68), channel_id=1, source_target_pairs={{0,28},{4,0},{8,4},{12,8},{16,12},{20,16},{24,20},{28,24},{1,29},{... | collective-permute-start | bytes 53768 | tf_op jit(solution)/shard_map/ppermute | solution.py:21
  10.2 0.7 copy.134
  10.8 2.9 %collective-permute-start = (bf16[7,5,1,1024]{3,0,2,1:T(8,128)(2,1)}, bf16[7,5,1,1024]{3,0,2,1:T(8,128)(2,1)}, u32[]{:S(2)}, u32[]{:S(2)}) collective-permute-start(bf16[7,5,1,1024]{3,0,2,1:T(8,128)(2,1)} %copy.134), channel_id=1, source_target_pairs={{1,0},{2,1},{3,2},{5,4},{6,5},{7,6},{9,8},{10,9},{11,10},{13,12},{... | collective-permute-start | bytes 215048 | tf_op jit(solution)/shard_map/ppermute | solution.py:15
  13.8 1.7 %fusion = f32[2048,140]{0,1:T(8,128)S(1)} fusion(bf16[140,1024]{1,0:T(8,128)(2,1)S(1)} %reshape_reshape.2, s32[2048]{0:T(1024)S(1)} %bitcast.128), kind=kOutput, calls=%fused_computation.3 | convolution fusion | flops 589299712 | bytes 1441792 | tf_op jit(solution)/shard_map/dot_general | solution.py:52
  15.5 2.8 %add_bitcast_fusion = (f32[140,2048]{1,0:T(8,128)S(1)}, f32[140,2048]{1,0:T(8,128)}) fusion(f32[2048,140]{0,1:T(8,128)S(1)} %fusion, bf16[140,1024]{1,0:T(8,128)(2,1)S(1)} %reshape_reshape.2, s32[2048]{0:T(1024)S(1)} %bitcast.124), kind=kOutput, calls=%fused_computation.36 | convolution fusion | flops 589873152 | bytes 3735552 | tf_op jit(solution)/shard_map/dot_general | solution.py:52
  18.2 0.3 add.64
  18.6 1.8 %sub.47 = f32[7,5,4,2048]{3,2,1,0:T(4,128)S(1)} reshape(f32[140,2048]{1,0:T(8,128)} %get-tuple-element.7) | data formatting | bytes 2293760 | tf_op jit(solution)/shard_map/sub | solution.py:38
  20.4 0.6 fusion.77
  21.0 3.0 %fusion.15 = f32[7,5,4,2048]{3,1,2,0:T(8,128)S(1)} fusion(f32[7,5,4,2048]{3,2,1,0:T(4,128)S(1)} %sub.47, f32[7,5,4,2048]{3,2,1,0:T(4,128)S(1)} %add.64, f32[4,2048]{1,0:T(4,128)S(1)} %multiply_bitcast_fusion, f32[1,5,5]{2,0,1:T(1,128)S(1)} %get-tuple-element.10), kind=kOutput, calls=%fused_computation.21 | convolution fusion | flops 18063360 | bytes 3473508 | tf_op jit(solution)/shard_map/vw,nw...->nv.../dot_general | solution.py:39
  24.0 0.7 copy.55
  24.8 0.4 reshape.68
  25.2 3.4 %fusion.2 = f32[140,1024]{1,0:T(8,128)} fusion(s32[2048]{0:T(1024)S(1)} %bitcast.129, s32[2048]{0:T(1024)S(1)} %bitcast.125, f32[140,2048]{1,0:T(8,128)S(1)} %reshape.68), kind=kOutput, calls=%fused_computation.6 | convolution fusion | flops 601792512 | bytes 1736704 | tf_op jit(solution)/shard_map/dot_general | solution.py:68
  28.6 3.4 %fusion.3 = f32[140,1024]{1,0:T(8,128)} fusion(s32[2048]{0:T(1024)S(1)} %bitcast.130, s32[2048]{0:T(1024)S(1)} %bitcast.126, f32[140,2048]{1,0:T(8,128)S(1)} %reshape.68), kind=kOutput, calls=%fused_computation.7 | convolution fusion | flops 600932352 | bytes 1736704 | tf_op jit(solution)/shard_map/dot_general | solution.py:65
  32.0 0.2 convolution_bitcast_fusion
  32.3 0.2 iota_compare_fusion.8
  32.9 0.8 fusion.25
  33.7 0.2 fusion.65
  34.0 5.6 %psum.7 = f32[1,3,7]{2,1,0:T(4,128)S(1)} all-reduce(f32[1,3,7]{2,1,0:T(4,128)S(1)} %convolution_bitcast_fusion.3), channel_id=1, replica_groups=mesh['circ'=8,'cell'=4] {'cell'}, use_global_device_ids=true, to_apply=%region_0.0 | all-reduce | flops 21 | bytes 168 | tf_op jit(solution)/shard_map/psum | solution.py:162
  39.6 21.7 %all_gather.3 = f32[8,3,7]{2,1,0:T(4,128)S(1)} all-gather(f32[1,3,7]{2,1,0:T(4,128)S(1)} %psum.7), channel_id=1, replica_groups=mesh['circ'=8,'cell'=4] {'circ'}, dimensions={0}, use_global_device_ids=true | all-gather | bytes 756 | tf_op jit(solution)/shard_map/all_gather | solution.py:163
  61.4 0.2 fusion.49
  61.5 0.2 convolution_negate_fusion
  61.8 3.9 %fusion.22 = f32[140,1024]{1,0:T(8,128)S(1)} fusion(f32[140,1024]{1,0:T(8,128)} %fusion.2, f32[140,1024]{1,0:T(8,128)} %fusion.3, s32[2048]{0:T(1024)S(1)} %bitcast.131, s32[2048]{0:T(1024)S(1)} %bitcast.127, f32[140,2048]{1,0:T(8,128)S(1)} %reshape.68), kind=kOutput, calls=%fused_computation.32 | convolution fusion | flops 600358912 | bytes 2883584 | tf_op jit(solution)/shard_map/dot_general | solution.py:64
  65.7 0.2 convolution_bitcast_fusion.2
  66.0 0.8 fusion.27
  66.9 1.1 %fusion.78 = (bf16[7,5,4,64]{3,1,2,0:T(8,128)(2,1)S(1)}, f32[7,5,4,64]{3,1,2,0:T(8,128)S(1)}) fusion(f32[7,5,4,64]{3,2,1,0:T(4,128)S(1)} %reshape.70, bf16[7,5,4,64]{3,1,2,0:T(8,128)(2,1)} %collective-permute-done.2, f32[4,64]{1,0:T(4,128)S(1)} %multiply_bitcast_fusion.2, f32[1,5,5]{2,0,1:T(1,128)S(1)} %copy-done.3), kind=kOutput, calls=%fused_computation.123 | convolution fusion | flops 609280 | bytes 108644 | tf_op jit(solution)/shard_map/vw,nw...->nv.../dot_general | solution.py:39
  68.2 0.2 reshape.69
  68.4 0.3 copy.59
  68.7 5.2 %collective-permute-done.3 = bf16[7,5,4,64]{3,1,2,0:T(8,128)(2,1)S(1)} collective-permute-done((bf16[7,5,4,64]{3,1,2,0:T(8,128)(2,1)S(1)}, bf16[7,5,4,64]{3,1,2,0:T(8,128)(2,1)S(1)}, u32[]{:S(2)}, u32[]{:S(2)}) %collective-permute-start.3) | collective-permute-done | bytes 17952 | tf_op jit(solution)/shard_map/ppermute | solution.py:21
  74.0 0.4 fusion.41
  74.4 0.4 convolution_add_fusion.1
  74.9 1.0 %copy.61 = f32[7,5,1,1024]{3,2,1,0:T(1,128)S(1)} copy(bf16[7,5,1,1024]{3,0,2,1:T(8,128)(2,1)} %collective-permute-done) | data formatting | bytes 215040 | tf_op jit(solution)/shard_map/convert_element_type | solution.py:122
  75.9 0.3 maximum_add_fusion
  76.2 1.2 %fusion.28 = f32[7,4,1024,5]{2,3,1,0:T(8,128)S(1)} fusion(f32[7,5,4,1024]{3,2,1,0:T(4,128)S(1)} %bitcast.117, f32[1,5,5]{2,0,1:T(1,128)S(1)} %get-tuple-element.11), kind=kOutput, calls=%fused_computation.49 | convolution fusion | flops 8601600 | bytes 1146980 | tf_op jit(solution)/shard_map/vw,nw...->nv.../dot_general | solution.py:39
  77.4 0.9 convert_element_type.116
  78.3 0.5 fusion.34
  78.8 0.6 slice.70
  79.5 10.1 %collective-permute-start.1 = (bf16[7,5,1,1024]{3,0,2,1:T(8,128)(2,1)}, bf16[7,5,1,1024]{3,0,2,1:T(8,128)(2,1)S(1)}, u32[]{:S(2)}, u32[]{:S(2)}) collective-permute-start(bf16[7,5,1,1024]{3,0,2,1:T(8,128)(2,1)} %slice.70), channel_id=1, source_target_pairs={{0,1},{1,2},{2,3},{4,5},{5,6},{6,7},{8,9},{9,10},{10,11},{12,13},{... | collective-permute-start | bytes 215048 | tf_op jit(solution)/shard_map/ppermute | solution.py:15
  89.5 0.4 convolution_add_fusion
  89.9 0.2 reshape.72
  90.1 1.2 %collective-permute-done.1 = bf16[7,5,1,1024]{3,0,2,1:T(8,128)(2,1)S(1)} collective-permute-done((bf16[7,5,1,1024]{3,0,2,1:T(8,128)(2,1)}, bf16[7,5,1,1024]{3,0,2,1:T(8,128)(2,1)S(1)}, u32[]{:S(2)}, u32[]{:S(2)}) %collective-permute-start.1) | collective-permute-done | bytes 71712 | tf_op jit(solution)/shard_map/ppermute | solution.py:15
  91.3 1.1 %fusion.35 = bf16[7,5,4,1024]{3,0,2,1:T(8,128)(2,1)S(1)} fusion(f32[7,5,4,1024]{3,2,1,0:T(4,128)S(1)} %reshape.72, f32[7,5,4,1024]{3,0,2,1:T(8,128)S(1)} %fusion.34, f32[7,5,4,1024]{3,2,1,0:T(4,128)S(1)} %reshape.69, f32[7,7,1,1]{1,0,3,2:T(8,128)S(1)} %copy-done.13, f32[7,5,3,1024]{3,0,2,1:T(8,128)S(1)} %slice.57, ...), kind=kOutput, calls=%fused_computation.57 | convolution fusion | flops 13189120 | bytes 2812100 | tf_op jit(solution)/shard_map/nm,mvac->nvac/dot_general | solution.py:104
  92.4 1.0 %copy.74 = bf16[7,5,4,1024]{3,2,1,0:T(4,128)(2,1)} copy(bf16[7,5,4,1024]{3,0,2,1:T(8,128)(2,1)S(1)} %fusion.35) | data formatting | bytes 573440 | tf_op jit(solution)/shard_map/convert_element_type | solution.py:150
  (58 shorter events, 1.3 us)
Async XLA Ops:
  0.6 33.3 %copy-start = (f32[3,256]{1,0:T(4,128)S(1)}, f32[3,256]{1,0:T(4,128)}, u32[]{:S(2)}) copy-start(f32[3,256]{1,0:T(4,128)} %param.24) | copy-start | bytes 9220
  0.6 9.4 %copy-start.1 = (bf16[35,1,4,1024]{3,2,1,0:T(4,128)(2,1)S(1)}, bf16[35,1,4,1024]{3,2,1,0:T(4,128)(2,1)}, u32[]{:S(2)}) copy-start(bf16[35,1,4,1024]{3,2,1,0:T(4,128)(2,1)} %param.14) | copy-start | bytes 860164
  0.7 13.1 %copy-start.6 = (s32[2,2048]{1,0:T(2,128)S(1)}, s32[2,2048]{1,0:T(2,128)}, u32[]{:S(2)}) copy-start(s32[2,2048]{1,0:T(2,128)} %param.20) | copy-start | bytes 49156
  5.0 61.9 %collective-permute-start.2 = (bf16[7,5,4,64]{3,1,2,0:T(8,128)(2,1)}, bf16[7,5,4,64]{3,1,2,0:T(8,128)(2,1)}, u32[]{:S(2)}, u32[]{:S(2)}) collective-permute-start(bf16[7,5,4,64]{3,1,2,0:T(8,128)(2,1)} %copy.68), channel_id=1, source_target_pairs={{0,28},{4,0},{8,4},{12,8},{16,12},{20,16},{24,20},{28,24},{1,29},{... | collective-permute-start | bytes 53768 | tf_op jit(solution)/shard_map/ppermute | solution.py:21
  10.8 64.0 %collective-permute-start = (bf16[7,5,1,1024]{3,0,2,1:T(8,128)(2,1)}, bf16[7,5,1,1024]{3,0,2,1:T(8,128)(2,1)}, u32[]{:S(2)}, u32[]{:S(2)}) collective-permute-start(bf16[7,5,1,1024]{3,0,2,1:T(8,128)(2,1)} %copy.134), channel_id=1, source_target_pairs={{1,0},{2,1},{3,2},{5,4},{6,5},{7,6},{9,8},{10,9},{11,10},{13,12},{... | collective-permute-start | bytes 215048 | tf_op jit(solution)/shard_map/ppermute | solution.py:15
  13.7 14.9 %copy-start.8 = (s32[1,2048]{1,0:T(1,128)}, s32[1,2048]{1,0:T(1,128)S(1)}, u32[]{:S(2)}) copy-start(s32[1,2048]{1,0:T(1,128)S(1)} %get-tuple-element.8) | copy-start | bytes 24580
  13.8 14.9 %copy-start.10 = (s32[1,2048]{1,0:T(1,128)}, s32[1,2048]{1,0:T(1,128)S(1)}, u32[]{:S(2)}) copy-start(s32[1,2048]{1,0:T(1,128)S(1)} %get-tuple-element.9) | copy-start | bytes 24580
  18.2 2.2 %copy-start.12 = (f32[3,5,5]{2,0,1:T(4,128)S(1)}, f32[3,5,5]{2,0,1:T(4,128)}, u32[]{:S(2)}) copy-start(f32[3,5,5]{2,0,1:T(4,128)} %param.19) | copy-start | bytes 904
  18.2 2.8 %copy-start.5 = (bf16[1,4,2048]{2,1,0:T(4,128)(2,1)S(1)}, bf16[1,4,2048]{2,1,0:T(4,128)(2,1)}, u32[]{:S(2)}) copy-start(bf16[1,4,2048]{2,1,0:T(4,128)(2,1)} %param.17) | copy-start | bytes 49156
  32.0 0.8 copy-start.16
  32.5 1.2 %copy-start.15 = (f32[5]{0:T(128)S(1)}, f32[5]{0:T(128)}, u32[]{:S(2)}) copy-start(f32[5]{0:T(128)} %param.25) | copy-start | bytes 64
  32.5 29.3 %copy-start.9 = (s32[1,2048]{1,0:T(1,128)S(1)}, s32[1,2048]{1,0:T(1,128)}, u32[]{:S(2)}) copy-start(s32[1,2048]{1,0:T(1,128)} %copy-done.8) | copy-start | bytes 24580
  32.5 29.3 %copy-start.11 = (s32[1,2048]{1,0:T(1,128)S(1)}, s32[1,2048]{1,0:T(1,128)}, u32[]{:S(2)}) copy-start(s32[1,2048]{1,0:T(1,128)} %copy-done.10) | copy-start | bytes 24580
  61.8 4.0 %copy-start.2 = (f32[2,8,3,400]{3,1,2,0:T(8,128)S(1)}, f32[2,8,3,400]{3,1,2,0:T(8,128)}, u32[]{:S(2)}) copy-start(f32[2,8,3,400]{3,1,2,0:T(8,128)} %param.26) | copy-start | bytes 230404
  61.8 5.0 %copy-start.14 = (bf16[1,4,64]{2,1,0:T(4,128)(2,1)S(1)}, bf16[1,4,64]{2,1,0:T(4,128)(2,1)}, u32[]{:S(2)}) copy-start(bf16[1,4,64]{2,1,0:T(4,128)(2,1)} %param.18) | copy-start | bytes 1540
  61.8 5.1 %copy-start.3 = (f32[1,5,5]{2,0,1:T(1,128)S(1)}, f32[1,5,5]{2,0,1:T(1,128)}, u32[]{:S(2)}) copy-start(f32[1,5,5]{2,0,1:T(1,128)} %get-tuple-element.12) | copy-start | bytes 304
  61.8 6.3 %copy-start.7 = (bf16[1,4,1024]{2,1,0:T(4,128)(2,1)S(1)}, bf16[1,4,1024]{2,1,0:T(4,128)(2,1)}, u32[]{:S(2)}) copy-start(bf16[1,4,1024]{2,1,0:T(4,128)(2,1)} %param.16) | copy-start | bytes 24580
  68.1 5.8 %collective-permute-start.3 = (bf16[7,5,4,64]{3,1,2,0:T(8,128)(2,1)S(1)}, bf16[7,5,4,64]{3,1,2,0:T(8,128)(2,1)S(1)}, u32[]{:S(2)}, u32[]{:S(2)}) collective-permute-start(bf16[7,5,4,64]{3,1,2,0:T(8,128)(2,1)S(1)} %get-tuple-element.15), channel_id=1, source_target_pairs={{0,4},{4,8},{8,12},{12,16},{16,20},{20,24},{24,28},{28,0},{1,5},{5... | collective-permute-start | bytes 53768 | tf_op jit(solution)/shard_map/ppermute | solution.py:21
  79.5 11.8 %copy-start.4 = (f32[1,4,1024]{2,1,0:T(4,128)S(1)}, f32[1,4,1024]{2,1,0:T(4,128)}, u32[]{:S(2)}) copy-start(f32[1,4,1024]{2,1,0:T(4,128)} %param.15) | copy-start | bytes 49156
  79.5 11.8 %copy-start.13 = (f32[7,7,1,1]{1,0,3,2:T(8,128)S(1)}, f32[7,7,1,1]{1,0,3,2:T(8,128)}, u32[]{:S(2)}) copy-start(f32[7,7,1,1]{1,0,3,2:T(8,128)} %constant.44) | copy-start | bytes 592
  79.5 11.8 %collective-permute-start.1 = (bf16[7,5,1,1024]{3,0,2,1:T(8,128)(2,1)}, bf16[7,5,1,1024]{3,0,2,1:T(8,128)(2,1)S(1)}, u32[]{:S(2)}, u32[]{:S(2)}) collective-permute-start(bf16[7,5,1,1024]{3,0,2,1:T(8,128)(2,1)} %slice.70), channel_id=1, source_target_pairs={{0,1},{1,2},{2,3},{4,5},{5,6},{6,7},{8,9},{9,10},{10,11},{12,13},{... | collective-permute-start | bytes 215048 | tf_op jit(solution)/shard_map/ppermute | solution.py:15
where the time goes:
time: 93.8 us; the launch traced here: 93.3 us
  blocking collectives  27.3 us (29%)
  matrix products  25.9 us (28%)
  starting transfers between devices  18 us (19%)
  local copies, waits for them, and re-layouts  11.8 us (13%)
  waiting for transfers between devices  6.34 us (7%)
  other arithmetic  2.79 us (3%)
  between operations  1.13 us (1%)
    all_gather x1, blocking collectives, shards(): all_forces = lax.all_gather(passage_force[None], 'circ', axis=0, tiled=True)  21.7 us
    ppermute x2, starting transfers between devices, shifted(): lax.ppermute(value, axis, [(source, source + steps) for source in range(f...  12.9 us
    dot_general x5, matrix products, take_columns(): picked = jnp.dot(flat_values, table, preferred_element_type=jnp.float32)  5.8 us
    psum x1, blocking collectives, shards(): passage_force = lax.psum(block_force, 'cell')  5.59 us
    dot_general x3, matrix products, face_flux(): jnp.einsum('vw,nw...->nv...', jacobian, total_state, precision=lax.Precis...  5.32 us
    ppermute x2, waiting for transfers between devices, shifted_2(): return lax.ppermute(value, axis, pairs)  5.17 us
    ppermute x2, starting transfers between devices, shifted_2(): return lax.ppermute(value, axis, pairs)  5.13 us
    dot_general x2, matrix products, spread_columns(): lax.dot_general(high_part, table, contract, preferred_element_type=jnp.fl...  4.3 us
  transfers between devices with their start and end apart: 4, of which 2 were waited for; matrix products, arithmetic and copies ran while one was open for 32% of the time, Pallas kernels for 0%

commit v1 on v0

--- a/solution.py
+++ b/solution.py
@@ -7,6 +7,18 @@
 
 NV = 5
 HB = 7
+
+
+def gather_by_bits(x, axis, dim):
+    ways, here, step = (lax.axis_size(axis), lax.axis_index(axis), x.shape[dim])
+    line, have = (x, 1)
+    while have < ways:
+        line = jnp.concatenate(
+            [line, lax.ppermute(line, axis, [(d, (d - have) % ways) for d in range(ways)])],
+            axis=dim,
+        )
+        have = 2 * have
+    return jnp.roll(line, here * step, axis=dim)
 
 
 def shifted(value, axis, steps):
@@ -160,7 +172,7 @@
     angle_step = 2.0 * math.pi / passages
     diameters = lax.iota(jnp.int32, passages)
     passage_force = lax.psum(block_force, "cell")
-    all_forces = lax.all_gather(passage_force[None], "circ", axis=0, tiled=True)
+    all_forces = gather_by_bits(passage_force[None], "circ", 0)
     modal_forces = project_all(all_forces, mode_shapes, passages, angle_step, diameters)
     return (jacobian_image, modal_forces)
 

time: 93.8 us -> 74 us (0.79)
  blocking collectives: 27.3 us -> 5.1 us
  waiting for transfers between devices: 6.34 us -> 10.5 us
  local copies, waits for them, and re-layouts: 11.8 us -> 10.1 us
  matrix products: 25.9 us -> 27 us
    all_gather x1 -> x0, blocking collectives: 21.7 us -> none  [shards(): all_forces = lax.all_gather(passage_force[None], 'circ', axis=0, tiled=True)]
    ppermute x0 -> x3, waiting for transfers between devices: none -> 5.63 us  [gather_by_bits(): lax.ppermute(line, axis, [(d, (d - have) % ways) for d in range(ways)])]
    ppermute x2, starting transfers between devices: 12.9 us -> 10.9 us  [shifted(): lax.ppermute(value, axis, [(source, source + steps) for source in range(f...]
    ppermute x2, waiting for transfers between devices: 5.17 us -> 3.69 us  [shifted_2(): return lax.ppermute(value, axis, pairs)]
    ppermute x2, starting transfers between devices: 5.13 us -> 6.34 us  [shifted_2(): return lax.ppermute(value, axis, pairs)]
  transfers between devices with their start and end apart: 4 -> 7, of which waited for: 2 -> 4; matrix products, arithmetic and copies ran while one was open for 32% -> 39% of each run, Pallas kernels for 0% -> 0%
where the time goes in v1:
time: 74 us; the launch traced here: 73.5 us
  matrix products  27 us (36%)
  starting transfers between devices  17.8 us (24%)
  waiting for transfers between devices  10.5 us (14%)
  local copies, waits for them, and re-layouts  10.1 us (14%)
  blocking collectives  5.1 us (7%)
  other arithmetic  1.93 us (3%)
  between operations  1.13 us (2%)
    ppermute x2, starting transfers between devices, shifted(): lax.ppermute(value, axis, [(source, source + steps) for source in range(f...  10.9 us
    ppermute x2, starting transfers between devices, shifted_2(): return lax.ppermute(value, axis, pairs)  6.34 us
    dot_general x5, matrix products, take_columns(): picked = jnp.dot(flat_values, table, preferred_element_type=jnp.float32)  5.8 us
    ppermute x3, waiting for transfers between devices, gather_by_bits(): lax.ppermute(line, axis, [(d, (d - have) % ways) for d in range(ways)])  5.63 us
    dot_general x3, matrix products, face_flux(): jnp.einsum('vw,nw...->nv...', jacobian, total_state, precision=lax.Precis...  5.34 us
    psum x1, blocking collectives, shards(): passage_force = lax.psum(block_force, 'cell')  5.1 us
    dot_general x2, matrix products, spread_columns(): lax.dot_general(high_part, table, contract, preferred_element_type=jnp.fl...  4.47 us
    dot_general x2, matrix products, spread_columns(): lax.dot_general(middle_part, table, contract, preferred_element_type=jnp....  3.83 us
  transfers between devices with their start and end apart: 7, of which 4 were waited for; matrix products, arithmetic and copies ran while one was open for 39% of the time, Pallas kernels for 0%

profile of v1, /device:TPU:1, one launch (start us, length us, event | category | flops | bytes accessed | tf_op | source)
XLA Modules:
  0.0 73.5 jit_solution(11965871670057080842)
XLA Ops:
  0.7 1.1 %reshape_reshape.2 = bf16[140,1024]{1,0:T(8,128)(2,1)S(1)} reshape(bf16[35,1,4,1024]{3,2,1,0:T(4,128)(2,1)} %param.14) | data formatting | bytes 573440 | tf_op jit(solution)/shard_map/reshape;reshape | solution.py:63
  1.8 0.8 %slice_bitcast_fusion.1 = (s32[64]{0:T(128)S(1)}, s32[64]{0:T(128)S(1)}) fusion(s32[2,64]{1,0:T(2,128)} %param.21), kind=kLoop, calls=%fused_computation.112 | loop fusion | bytes 1024 | tf_op jit(solution)/shard_map/eq | solution.py:58
  2.5 0.7 compare_select_fusion
  3.2 0.8 %gather_fusion = s32[64]{0:T(128)S(1)} fusion(s32[64]{0:T(128)S(1)} %get-tuple-element.16, s32[1024]{0:T(1024)S(1)} %pad_clamp_fusion), kind=kCustom, calls=%fused_computation | custom fusion | bytes 768 | tf_op jit(solution)/shard_map/gather | solution.py:146
  4.0 0.3 fusion.26
  4.4 0.6 copy.104
  5.0 5.1 %collective-permute-start.2 = (bf16[7,5,4,64]{3,1,2,0:T(8,128)(2,1)}, bf16[7,5,4,64]{3,1,2,0:T(8,128)(2,1)}, u32[]{:S(2)}, u32[]{:S(2)}) collective-permute-start(bf16[7,5,4,64]{3,1,2,0:T(8,128)(2,1)} %copy.104), channel_id=1, source_target_pairs={{0,28},{4,0},{8,4},{12,8},{16,12},{20,16},{24,20},{28,24},{1,29},{... | collective-permute-start | bytes 53768 | tf_op jit(solution)/shard_map/ppermute | solution.py:33
  10.2 2.9 %collective-permute-start = (bf16[7,5,1,1024]{3,0,2,1:T(8,128)(2,1)S(1)}, bf16[7,5,1,1024]{3,0,2,1:T(8,128)(2,1)S(1)}, u32[]{:S(2)}, u32[]{:S(2)}) collective-permute-start(bf16[7,5,1,1024]{3,0,2,1:T(8,128)(2,1)S(1)} %copy.165), channel_id=1, source_target_pairs={{1,0},{2,1},{3,2},{5,4},{6,5},{7,6},{9,8},{10,9},{11,10},{13,12},{... | collective-permute-start | bytes 215048 | tf_op jit(solution)/shard_map/ppermute | solution.py:27
  13.4 0.8 %fusion.25 = f32[35,256]{1,0:T(8,128)S(1)} fusion(bf16[35,4096]{1,0:T(8,128)(2,1)S(1)} %bitcast.121, s32[256]{0:T(256)S(1)} %copy-done.11), kind=kOutput, calls=%fused_computation.42 | convolution fusion | flops 74448896 | bytes 323584 | tf_op jit(solution)/shard_map/dot_general | solution.py:64
  14.2 0.2 fusion.65
  14.5 5.1 %psum.7 = f32[1,3,7]{2,0,1:T(1,128)S(1)} all-reduce(f32[1,3,7]{2,0,1:T(1,128)S(1)} %copy.111), channel_id=1, replica_groups=mesh['circ'=8,'cell'=4] {'cell'}, use_global_device_ids=true, to_apply=%region_0.0 | all-reduce | flops 21 | bytes 168 | tf_op jit(solution)/shard_map/psum | solution.py:174
  19.6 0.3 collective-permute-start.4
  19.9 1.7 %fusion = f32[2048,140]{0,1:T(8,128)S(1)} fusion(bf16[140,1024]{1,0:T(8,128)(2,1)S(1)} %reshape_reshape.2, s32[2048]{0:T(1024)S(1)} %bitcast.128), kind=kOutput, calls=%fused_computation.3 | convolution fusion | flops 589299712 | bytes 1441792 | tf_op jit(solution)/shard_map/dot_general | solution.py:64
  21.6 2.8 %add_bitcast_fusion = (f32[140,2048]{1,0:T(8,128)S(1)}, f32[140,2048]{1,0:T(8,128)}) fusion(f32[2048,140]{0,1:T(8,128)S(1)} %fusion, bf16[140,1024]{1,0:T(8,128)(2,1)S(1)} %reshape_reshape.2, s32[2048]{0:T(1024)S(1)} %bitcast.124), kind=kOutput, calls=%fused_computation.36 | convolution fusion | flops 589873152 | bytes 3735552 | tf_op jit(solution)/shard_map/dot_general | solution.py:64
  24.4 0.3 add.74
  24.8 1.8 %sub.51 = f32[7,5,4,2048]{3,2,1,0:T(4,128)S(1)} reshape(f32[140,2048]{1,0:T(8,128)} %get-tuple-element.9) | data formatting | bytes 2293760 | tf_op jit(solution)/shard_map/sub | solution.py:50
  26.6 3.0 %fusion.15 = f32[7,5,4,2048]{3,1,2,0:T(8,128)S(1)} fusion(f32[7,5,4,2048]{3,2,1,0:T(4,128)S(1)} %sub.51, f32[7,5,4,2048]{3,2,1,0:T(4,128)S(1)} %add.74, f32[4,2048]{1,0:T(4,128)S(1)} %multiply_bitcast_fusion, f32[1,5,5]{2,0,1:T(1,128)S(1)} %get-tuple-element.12), kind=kOutput, calls=%fused_computation.21 | convolution fusion | flops 18063360 | bytes 3473508 | tf_op jit(solution)/shard_map/vw,nw...->nv.../dot_general | solution.py:51
  29.6 0.7 %copy.91 = f32[7,5,4,2048]{3,2,1,0:T(4,128)S(1)} copy(f32[7,5,4,2048]{3,1,2,0:T(8,128)S(1)} %fusion.15) | data formatting | bytes 2293760 | tf_op jit(solution)/shard_map/sub | solution.py:54
  30.4 0.4 reshape.68
  30.8 3.4 %fusion.2 = f32[140,1024]{1,0:T(8,128)} fusion(s32[2048]{0:T(1024)S(1)} %bitcast.129, s32[2048]{0:T(1024)S(1)} %bitcast.125, f32[140,2048]{1,0:T(8,128)S(1)} %reshape.68), kind=kOutput, calls=%fused_computation.6 | convolution fusion | flops 601792512 | bytes 1736704 | tf_op jit(solution)/shard_map/dot_general | solution.py:80
  34.2 3.4 %fusion.3 = f32[140,1024]{1,0:T(8,128)} fusion(s32[2048]{0:T(1024)S(1)} %bitcast.130, s32[2048]{0:T(1024)S(1)} %bitcast.126, f32[140,2048]{1,0:T(8,128)S(1)} %reshape.68), kind=kOutput, calls=%fused_computation.7 | convolution fusion | flops 600932352 | bytes 1736704 | tf_op jit(solution)/shard_map/dot_general | solution.py:77
  37.6 0.2 convolution_bitcast_fusion
  38.2 4.1 %fusion.22 = f32[140,1024]{1,0:T(8,128)S(1)} fusion(f32[140,1024]{1,0:T(8,128)} %fusion.2, f32[140,1024]{1,0:T(8,128)} %fusion.3, s32[2048]{0:T(1024)S(1)} %bitcast.131, s32[2048]{0:T(1024)S(1)} %bitcast.127, f32[140,2048]{1,0:T(8,128)S(1)} %reshape.68), kind=kOutput, calls=%fused_computation.32 | convolution fusion | flops 600358912 | bytes 2883584 | tf_op jit(solution)/shard_map/dot_general | solution.py:76
  42.3 0.2 reshape.69
  42.6 0.3 copy-done.6
  43.0 0.3 copy.95
  43.3 0.2 collective-permute-start.5
  43.5 2.3 %collective-permute-done.5 = f32[2,3,7]{2,0,1:T(2,128)S(1)} collective-permute-done((f32[2,3,7]{2,0,1:T(2,128)S(1)}, f32[2,3,7]{2,0,1:T(2,128)S(1)}, u32[]{:S(2)}, u32[]{:S(2)}) %collective-permute-start.5) | collective-permute-done | bytes 200 | tf_op jit(solution)/shard_map/ppermute | solution.py:17
  45.9 3.4 %collective-permute-done.6 = f32[4,3,7]{2,0,1:T(4,128)S(1)} collective-permute-done((f32[4,3,7]{2,0,1:T(4,128)S(1)}, f32[4,3,7]{2,0,1:T(4,128)S(1)}, u32[]{:S(2)}, u32[]{:S(2)}) %collective-permute-start.6) | collective-permute-done | bytes 368 | tf_op jit(solution)/shard_map/ppermute | solution.py:17
  49.3 0.2 fusion.49
  49.5 0.2 convolution_bitcast_fusion.2
  49.8 0.2 convolution_negate_fusion
  49.9 1.2 %fusion.78 = (bf16[7,5,4,64]{3,1,2,0:T(8,128)(2,1)S(1)}, f32[7,5,4,64]{3,1,2,0:T(8,128)S(1)}) fusion(f32[7,5,4,64]{3,2,1,0:T(4,128)S(1)} %reshape.70, bf16[7,5,4,64]{3,1,2,0:T(8,128)(2,1)} %collective-permute-done.2, f32[4,64]{1,0:T(4,128)S(1)} %multiply_bitcast_fusion.2, f32[1,5,5]{2,0,1:T(1,128)S(1)} %get-tuple-element.14), kind=kOutput, calls=%fused_computation.125 | convolution fusion | flops 609280 | bytes 108644 | tf_op jit(solution)/shard_map/vw,nw...->nv.../dot_general | solution.py:51
  51.1 1.3 %collective-permute-start.3 = (bf16[7,5,4,64]{3,1,2,0:T(8,128)(2,1)S(1)}, bf16[7,5,4,64]{3,1,2,0:T(8,128)(2,1)S(1)}, u32[]{:S(2)}, u32[]{:S(2)}) collective-permute-start(bf16[7,5,4,64]{3,1,2,0:T(8,128)(2,1)S(1)} %get-tuple-element.17), channel_id=1, source_target_pairs={{0,4},{4,8},{8,12},{12,16},{16,20},{20,24},{24,28},{28,0},{1,5},{5... | collective-permute-start | bytes 53768 | tf_op jit(solution)/shard_map/ppermute | solution.py:33
  52.4 0.8 %fusion.27 = f32[7,400]{1,0:T(8,128)} fusion(f32[7,400]{1,0:T(8,128)S(1)} %convolution_bitcast_fusion.2, f32[8,3,7]{2,0,1:T(8,128)S(1)} %convolution_negate_fusion, f32[2,8,3,400]{3,1,2,0:T(8,128)S(1)} %copy-done.2), kind=kOutput, calls=%fused_computation.45 | convolution fusion | flops 809200 | bytes 89024 | tf_op jit(solution)/shard_map/dkm,dkn->nm/dot_general | solution.py:92
  53.2 3.7 %collective-permute-done.3 = bf16[7,5,4,64]{3,1,2,0:T(8,128)(2,1)S(1)} collective-permute-done((bf16[7,5,4,64]{3,1,2,0:T(8,128)(2,1)S(1)}, bf16[7,5,4,64]{3,1,2,0:T(8,128)(2,1)S(1)}, u32[]{:S(2)}, u32[]{:S(2)}) %collective-permute-start.3) | collective-permute-done | bytes 17952 | tf_op jit(solution)/shard_map/ppermute | solution.py:33
  57.1 0.4 fusion.41
  57.5 0.4 convolution_add_fusion.1
  58.0 0.3 maximum_add_fusion
  58.3 1.2 %fusion.28 = f32[7,4,1024,5]{2,3,1,0:T(8,128)S(1)} fusion(f32[7,5,4,1024]{3,2,1,0:T(4,128)S(1)} %bitcast.117, f32[1,5,5]{2,0,1:T(1,128)S(1)} %get-tuple-element.13), kind=kOutput, calls=%fused_computation.49 | convolution fusion | flops 8601600 | bytes 1146980 | tf_op jit(solution)/shard_map/vw,nw...->nv.../dot_general | solution.py:51
  59.5 0.5 fusion.34
  60.1 0.6 slice.70
  60.7 8.1 %collective-permute-start.1 = (bf16[7,5,1,1024]{3,0,2,1:T(8,128)(2,1)}, bf16[7,5,1,1024]{3,0,2,1:T(8,128)(2,1)}, u32[]{:S(2)}, u32[]{:S(2)}) collective-permute-start(bf16[7,5,1,1024]{3,0,2,1:T(8,128)(2,1)} %slice.70), channel_id=1, source_target_pairs={{0,1},{1,2},{2,3},{4,5},{5,6},{6,7},{8,9},{9,10},{10,11},{12,13},{... | collective-permute-start | bytes 215048 | tf_op jit(solution)/shard_map/ppermute | solution.py:27
  68.8 0.4 convolution_add_fusion
  69.2 0.2 reshape.72
  69.4 1.2 %collective-permute-done.1 = bf16[7,5,1,1024]{3,0,2,1:T(8,128)(2,1)} collective-permute-done((bf16[7,5,1,1024]{3,0,2,1:T(8,128)(2,1)}, bf16[7,5,1,1024]{3,0,2,1:T(8,128)(2,1)}, u32[]{:S(2)}, u32[]{:S(2)}) %collective-permute-start.1) | collective-permute-done | bytes 71712 | tf_op jit(solution)/shard_map/ppermute | solution.py:27
  70.6 2.0 %fusion.35 = bf16[7,5,4,1024]{3,0,2,1:T(8,128)(2,1)S(1)} fusion(f32[7,5,4,1024]{3,2,1,0:T(4,128)S(1)} %reshape.72, f32[7,5,4,1024]{3,0,2,1:T(8,128)S(1)} %fusion.34, f32[7,5,4,1024]{3,2,1,0:T(4,128)S(1)} %reshape.69, f32[7,7,1,1]{1,0,3,2:T(8,128)S(1)} %copy-done.8, f32[7,5,3,1024]{3,0,2,1:T(8,128)S(1)} %slice.57, ...), kind=kOutput, calls=%fused_computation.57 | convolution fusion | flops 13189120 | bytes 2812100 | tf_op jit(solution)/shard_map/nm,mvac->nvac/dot_general | solution.py:116
  72.6 1.0 %copy.110 = bf16[7,5,4,1024]{3,2,1,0:T(4,128)(2,1)} copy(bf16[7,5,4,1024]{3,0,2,1:T(8,128)(2,1)S(1)} %fusion.35) | data formatting | bytes 573440 | tf_op jit(solution)/shard_map/convert_element_type | solution.py:162
  (57 shorter events, 1.6 us)
Async XLA Ops:
  0.6 13.8 %copy-start = (f32[3,256]{1,0:T(4,128)S(1)}, f32[3,256]{1,0:T(4,128)}, u32[]{:S(2)}) copy-start(f32[3,256]{1,0:T(4,128)} %param.24) | copy-start | bytes 9220
  0.6 9.5 %copy-start.1 = (bf16[35,1,4,1024]{3,2,1,0:T(4,128)(2,1)S(1)}, bf16[35,1,4,1024]{3,2,1,0:T(4,128)(2,1)}, u32[]{:S(2)}) copy-start(bf16[35,1,4,1024]{3,2,1,0:T(4,128)(2,1)} %param.14) | copy-start | bytes 860164
  0.7 12.7 %copy-start.11 = (s32[256]{0:T(256)S(1)}, s32[256]{0:T(256)}, u32[]{:S(2)}) copy-start(s32[256]{0:T(256)} %param.23) | copy-start | bytes 3076
  4.2 10.0 %copy-start.10 = (f32[5]{0:T(128)S(1)}, f32[5]{0:T(128)}, u32[]{:S(2)}) copy-start(f32[5]{0:T(128)} %param.25) | copy-start | bytes 64
  4.2 15.7 %copy-start.5 = (s32[2,2048]{1,0:T(2,128)S(1)}, s32[2,2048]{1,0:T(2,128)}, u32[]{:S(2)}) copy-start(s32[2,2048]{1,0:T(2,128)} %param.20) | copy-start | bytes 49156
  5.0 44.9 %collective-permute-start.2 = (bf16[7,5,4,64]{3,1,2,0:T(8,128)(2,1)}, bf16[7,5,4,64]{3,1,2,0:T(8,128)(2,1)}, u32[]{:S(2)}, u32[]{:S(2)}) collective-permute-start(bf16[7,5,4,64]{3,1,2,0:T(8,128)(2,1)} %copy.104), channel_id=1, source_target_pairs={{0,28},{4,0},{8,4},{12,8},{16,12},{20,16},{24,20},{28,24},{1,29},{... | collective-permute-start | bytes 53768 | tf_op jit(solution)/shard_map/ppermute | solution.py:33
  10.2 47.6 %collective-permute-start = (bf16[7,5,1,1024]{3,0,2,1:T(8,128)(2,1)S(1)}, bf16[7,5,1,1024]{3,0,2,1:T(8,128)(2,1)S(1)}, u32[]{:S(2)}, u32[]{:S(2)}) collective-permute-start(bf16[7,5,1,1024]{3,0,2,1:T(8,128)(2,1)S(1)} %copy.165), channel_id=1, source_target_pairs={{1,0},{2,1},{3,2},{5,4},{6,5},{7,6},{9,8},{10,9},{11,10},{13,12},{... | collective-permute-start | bytes 215048 | tf_op jit(solution)/shard_map/ppermute | solution.py:27
  19.6 23.6 %collective-permute-start.4 = (f32[1,3,7]{2,0,1:T(1,128)S(1)}, f32[1,3,7]{2,0,1:T(1,128)S(1)}, u32[]{:S(2)}, u32[]{:S(2)}) collective-permute-start(f32[1,3,7]{2,0,1:T(1,128)S(1)} %psum.7), channel_id=1, source_target_pairs={{0,28},{4,0},{8,4},{12,8},{16,12},{20,16},{24,20},{28,24},{1,29},{... | collective-permute-start | bytes 260 | tf_op jit(solution)/shard_map/ppermute | solution.py:17
  24.4 2.2 %copy-start.7 = (f32[3,5,5]{2,0,1:T(4,128)S(1)}, f32[3,5,5]{2,0,1:T(4,128)}, u32[]{:S(2)}) copy-start(f32[3,5,5]{2,0,1:T(4,128)} %param.19) | copy-start | bytes 904
  24.4 2.2 %copy-start.4 = (bf16[1,4,2048]{2,1,0:T(4,128)(2,1)S(1)}, bf16[1,4,2048]{2,1,0:T(4,128)(2,1)}, u32[]{:S(2)}) copy-start(bf16[1,4,2048]{2,1,0:T(4,128)(2,1)} %param.17) | copy-start | bytes 49156
  38.2 4.4 %copy-start.9 = (bf16[1,4,64]{2,1,0:T(4,128)(2,1)S(1)}, bf16[1,4,64]{2,1,0:T(4,128)(2,1)}, u32[]{:S(2)}) copy-start(bf16[1,4,64]{2,1,0:T(4,128)(2,1)} %param.18) | copy-start | bytes 1540
  42.3 0.7 copy-start.6
  42.3 7.2 %copy-start.2 = (f32[2,8,3,400]{3,1,2,0:T(8,128)S(1)}, f32[2,8,3,400]{3,1,2,0:T(8,128)}, u32[]{:S(2)}) copy-start(f32[2,8,3,400]{3,1,2,0:T(8,128)} %param.26) | copy-start | bytes 230404
  43.3 2.5 %collective-permute-start.5 = (f32[2,3,7]{2,0,1:T(2,128)S(1)}, f32[2,3,7]{2,0,1:T(2,128)S(1)}, u32[]{:S(2)}, u32[]{:S(2)}) collective-permute-start(f32[2,3,7]{2,0,1:T(2,128)S(1)} %pad_maximum_fusion.2), channel_id=1, source_target_pairs={{0,24},{4,28},{8,0},{12,4},{16,8},{20,12},{24,16},{28,20},{1,25},{... | collective-permute-start | bytes 512 | tf_op jit(solution)/shard_map/ppermute | solution.py:17
  45.8 3.4 %collective-permute-start.6 = (f32[4,3,7]{2,0,1:T(4,128)S(1)}, f32[4,3,7]{2,0,1:T(4,128)S(1)}, u32[]{:S(2)}, u32[]{:S(2)}) collective-permute-start(f32[4,3,7]{2,0,1:T(4,128)S(1)} %pad_maximum_fusion.1), channel_id=1, source_target_pairs={{0,16},{4,20},{8,24},{12,28},{16,0},{20,4},{24,8},{28,12},{1,17},{... | collective-permute-start | bytes 1016 | tf_op jit(solution)/shard_map/ppermute | solution.py:17
  51.1 5.8 %collective-permute-start.3 = (bf16[7,5,4,64]{3,1,2,0:T(8,128)(2,1)S(1)}, bf16[7,5,4,64]{3,1,2,0:T(8,128)(2,1)S(1)}, u32[]{:S(2)}, u32[]{:S(2)}) collective-permute-start(bf16[7,5,4,64]{3,1,2,0:T(8,128)(2,1)S(1)} %get-tuple-element.17), channel_id=1, source_target_pairs={{0,4},{4,8},{8,12},{12,16},{16,20},{20,24},{24,28},{28,0},{1,5},{5... | collective-permute-start | bytes 53768 | tf_op jit(solution)/shard_map/ppermute | solution.py:33
  60.7 9.9 %copy-start.3 = (f32[1,4,1024]{2,1,0:T(4,128)S(1)}, f32[1,4,1024]{2,1,0:T(4,128)}, u32[]{:S(2)}) copy-start(f32[1,4,1024]{2,1,0:T(4,128)} %param.15) | copy-start | bytes 49156
  60.7 9.9 %copy-start.8 = (f32[7,7,1,1]{1,0,3,2:T(8,128)S(1)}, f32[7,7,1,1]{1,0,3,2:T(8,128)}, u32[]{:S(2)}) copy-start(f32[7,7,1,1]{1,0,3,2:T(8,128)} %constant.66) | copy-start | bytes 592
  60.7 9.8 %collective-permute-start.1 = (bf16[7,5,1,1024]{3,0,2,1:T(8,128)(2,1)}, bf16[7,5,1,1024]{3,0,2,1:T(8,128)(2,1)}, u32[]{:S(2)}, u32[]{:S(2)}) collective-permute-start(bf16[7,5,1,1024]{3,0,2,1:T(8,128)(2,1)} %slice.70), channel_id=1, source_target_pairs={{0,1},{1,2},{2,3},{4,5},{5,6},{6,7},{8,9},{9,10},{10,11},{12,13},{... | collective-permute-start | bytes 215048 | tf_op jit(solution)/shard_map/ppermute | solution.py:27
